TPU v7x, 128 devices: a whole 4x4x4 slice. The times are simulated.
128 devices in a mesh: row: 16 (over x, z), col: 8 (over y, core).
Axes of the slice: x: 4, y: 4, z: 4, core: 2. Of those that a mesh axis runs over, the one named last changes fastest.
Arguments:
- t_upper: bfloat16 [3, 4096, 4096], P(None, 'row', 'col'), may hold values from -0.03125 to 0.03125
- t_old: bfloat16 [3, 4096, 24576], P(None, 'row', 'col'), may hold values from -0.03125 to 0.03125
- inverses: bfloat16 [3, 4096, 4096], P(None, 'row', 'col'), may hold values from -1 to 1.5, as said below
- forcing: float32 [3, 4096, 128], P(None, 'row'), may hold values from -6 to 6
- x_old: bfloat16 [24576, 128], P('col'), may hold values from -6 to 6
- offsets: float32 [128], replicated, may hold values from -0.5 to 0.5
- starts: int32 [128], replicated, may hold values from 0 to 36864
- column_map: int32 [128], replicated, may hold values from 0 to 127, each once
- z_cols: bfloat16 [49152, 3, 4096], P('row', None, 'col'), may hold values from -0.0546875 to 0.0546875
- acc: float32 [49152, 128], P(('row', 'col')), may hold values from -6 to 6
Outputs:
- solved: float32 [3, 4096, 128], P(None, ('row', 'col'))
- acc_out: float32 [49152, 128], P(('row', 'col'))
Inputs may be any that keep to these rules, and one draw needn't show every extreme that they name: `inverses`: dense matrices with a dominant positive diagonal.
All inputs are finite; a program needn't handle non-finite values.
Results may differ from a plain program's by a relative error of at most 0.0003.
Values may be sent and summed in bfloat16 or wider, within the bound.
No kernel may reach another device: no remote copies, remote signals or barrier semaphores. Data moves between devices by JAX's collectives and lax.ppermute only.
A program may use at most 128 MiB of HBM per device.

v0:
```python
import jax
import jax.numpy as jnp
from jax import lax
from jax.sharding import PartitionSpec as P

NEUMANN = 3


def split_pair(values):
    upper = values.astype(jnp.bfloat16)
    lower = (values - lax.optimization_barrier(upper).astype(jnp.float32)).astype(jnp.bfloat16)
    return jnp.concatenate([upper, lower], axis=-1)


def body(t_upper, t_old, inverses, forcing, x_old, offsets, starts, column_map, z_cols, acc):
    n_col = lax.axis_size("col")
    row_idx = lax.axis_index("row")
    col_idx = lax.axis_index("col")
    steps = forcing.shape[0]
    row_block = t_upper.shape[1]
    col_block = t_upper.shape[2]
    width = forcing.shape[2]
    old_cols = x_old.shape[0]
    full_rows = col_block * n_col
    share = row_block // n_col
    pairs = {}
    count = 0
    for first in range(steps):
        for second in range(first + 1, steps):
            pairs[first, second] = count
            count = count + 1

    def fold_pair(product):
        return product[:, :width] + product[:, width:]

    old_rows = steps * full_rows + col_idx * old_cols + jnp.arange(old_cols, dtype=jnp.int32)
    old_live = old_rows[:, None] < starts[None, :]
    old_vals = jnp.where(old_live, x_old, jnp.zeros_like(x_old))
    local_start = row_idx * row_block

    def reduce_rows(partial_value):
        return lax.psum(partial_value, "col")

    def spread_rows(values):
        return lax.all_gather(values, "row", axis=0, tiled=True)

    def own_cols(whole):
        return lax.dynamic_slice_in_dim(whole, col_idx * col_block, col_block, 0)

    solved_full = {}
    pieces = {}
    for step in reversed(range(steps)):
        partial_value = -jnp.dot(t_old[step], old_vals, preferred_element_type=jnp.float32)
        for later in range(step + 1, steps):
            partial_value = partial_value - fold_pair(
                jnp.dot(
                    t_upper[pairs[step, later]],
                    own_cols(solved_full[later]),
                    preferred_element_type=jnp.float32,
                )
            )
        rhs = reduce_rows(partial_value) + forcing[step]
        gathered = spread_rows(split_pair(rhs))
        term = reduce_rows(
            fold_pair(
                jnp.dot(inverses[step], own_cols(gathered), preferred_element_type=jnp.float32)
            )
        )
        total = term
        for extra in range(1, NEUMANN):
            gathered = spread_rows(split_pair(term))
            term = (
                reduce_rows(
                    fold_pair(
                        jnp.dot(
                            inverses[step], own_cols(gathered), preferred_element_type=jnp.float32
                        )
                    )
                )
                * offsets[None, :]
            )
            total = total + term
        rows = step * full_rows + local_start + jnp.arange(row_block, dtype=jnp.int32)
        total = jnp.where(rows[:, None] < starts[None, :], total, jnp.zeros_like(total))
        pieces[step] = lax.dynamic_slice_in_dim(total, col_idx * share, share, 0)
        solved_full[step] = spread_rows(split_pair(total))
    stacked = jnp.concatenate([own_cols(solved_full[step]) for step in range(steps)], axis=0)
    one_hot = (jnp.arange(width, dtype=jnp.int32)[:, None] == column_map[None, :]).astype(
        jnp.bfloat16
    )
    picked_upper = jnp.dot(stacked[:, :width], one_hot, preferred_element_type=jnp.float32).astype(
        jnp.bfloat16
    )
    picked_lower = jnp.dot(stacked[:, width:], one_hot, preferred_element_type=jnp.float32).astype(
        jnp.bfloat16
    )
    picked = jnp.concatenate([picked_upper, picked_lower], axis=1)
    z_rows = z_cols.shape[0]
    z_flat = z_cols.reshape(z_rows, steps * col_block)
    contribution = lax.psum_scatter(
        fold_pair(jnp.dot(z_flat, picked, preferred_element_type=jnp.float32)),
        "col",
        scatter_dimension=0,
        tiled=True,
    )
    solved = jnp.stack([pieces[step] for step in range(steps)])
    return (solved, acc + contribution)


def solution(mesh):
    placed = (
        P(None, "row", "col"),
        P(None, "row", "col"),
        P(None, "row", "col"),
        P(None, "row", None),
        P("col", None),
        P(),
        P(),
        P(),
        P("row", None, "col"),
        P(("row", "col"), None),
    )
    return jax.shard_map(
        body,
        mesh=mesh,
        in_specs=placed,
        out_specs=(P(None, ("row", "col"), None), P(("row", "col"), None)),
        check_vma=False,
    )
```

profile of v0, /device:TPU:0, one launch (start us, length us, event | category | flops | bytes accessed | tf_op | source)
XLA Modules:
  0.0 1396.4 jit_solution(2241294068387488249)
XLA Ops:
  11.0 62.4 %all-reduce.13.cloned.1.call-done = f32[256,128]{0,1:T(8,128)} async-done(((f32[256,128]{0,1:T(8,128)}), f32[256,128]{0,1:T(8,128)}) %all-reduce.13.cloned.1.call-update) | async-done | bytes 131088 | tf_op jit(solution)/shard_map/psum | solution.py:42
  76.0 46.2 %all-gather.13.cloned.1.call-done = bf16[4096,256]{0,1:T(8,128)(2,1)} async-done(((bf16[256,256]{0,1:T(8,128)(2,1)}), bf16[4096,256]{0,1:T(8,128)(2,1)}) %all-gather.13.cloned.1.call-update) | async-done | bytes 2097168 | tf_op jit(solution)/shard_map/all_gather | solution.py:45
  124.2 60.2 %all-reduce.15.cloned.1.call-done = f32[256,128]{0,1:T(8,128)} async-done(((f32[256,128]{0,1:T(8,128)}), f32[256,128]{0,1:T(8,128)}) %all-reduce.15.cloned.1.call-update) | async-done | bytes 131088 | tf_op jit(solution)/shard_map/psum | solution.py:42
  187.0 46.2 %all-gather.15.cloned.1.call-done = bf16[4096,256]{0,1:T(8,128)(2,1)} async-done(((bf16[256,256]{0,1:T(8,128)(2,1)}), bf16[4096,256]{0,1:T(8,128)(2,1)}) %all-gather.15.cloned.1.call-update) | async-done | bytes 2097168 | tf_op jit(solution)/shard_map/all_gather | solution.py:45
  235.2 60.1 %all-reduce.17.cloned.1.call-done = f32[256,128]{0,1:T(8,128)} async-done(((f32[256,128]{0,1:T(8,128)}), f32[256,128]{0,1:T(8,128)}) %all-reduce.17.cloned.1.call-update) | async-done | bytes 131088 | tf_op jit(solution)/shard_map/psum | solution.py:42
  298.1 46.2 %all-gather.17.cloned.1.call-done = bf16[4096,256]{0,1:T(8,128)(2,1)} async-done(((bf16[256,256]{0,1:T(8,128)(2,1)}), bf16[4096,256]{0,1:T(8,128)(2,1)}) %all-gather.17.cloned.1.call-update) | async-done | bytes 2097168 | tf_op jit(solution)/shard_map/all_gather | solution.py:45
  346.3 60.2 %all-reduce.19.cloned.1.call-done = f32[256,128]{0,1:T(8,128)} async-done(((f32[256,128]{0,1:T(8,128)}), f32[256,128]{0,1:T(8,128)}) %all-reduce.19.cloned.1.call-update) | async-done | bytes 131088 | tf_op jit(solution)/shard_map/psum | solution.py:42
  408.3 47.0 %all-gather.19.cloned.1.call-done = bf16[4096,256]{0,1:T(8,128)(2,1)} async-done(((bf16[256,256]{0,1:T(8,128)(2,1)}), bf16[4096,256]{0,1:T(8,128)(2,1)}) %all-gather.19.cloned.1.call-update) | async-done | bytes 2097168 | tf_op jit(solution)/shard_map/all_gather | solution.py:45
  460.3 59.3 %all-reduce.21.cloned.1.call-done = f32[256,128]{0,1:T(8,128)} async-done(((f32[256,128]{0,1:T(8,128)}), f32[256,128]{0,1:T(8,128)}) %all-reduce.21.cloned.1.call-update) | async-done | bytes 131088 | tf_op jit(solution)/shard_map/psum | solution.py:42
  522.1 46.2 %all-gather.21.cloned.1.call-done = bf16[4096,256]{0,1:T(8,128)(2,1)} async-done(((bf16[256,256]{0,1:T(8,128)(2,1)}), bf16[4096,256]{0,1:T(8,128)(2,1)}) %all-gather.21.cloned.1.call-update) | async-done | bytes 2097168 | tf_op jit(solution)/shard_map/all_gather | solution.py:45
  570.3 60.2 %all-reduce.23.cloned.1.call-done = f32[256,128]{0,1:T(8,128)} async-done(((f32[256,128]{0,1:T(8,128)}), f32[256,128]{0,1:T(8,128)}) %all-reduce.23.cloned.1.call-update) | async-done | bytes 131088 | tf_op jit(solution)/shard_map/psum | solution.py:42
  633.2 46.2 %all-gather.23.cloned.1.call-done = bf16[4096,256]{0,1:T(8,128)(2,1)} async-done(((bf16[256,256]{0,1:T(8,128)(2,1)}), bf16[4096,256]{0,1:T(8,128)(2,1)}) %all-gather.23.cloned.1.call-update) | async-done | bytes 2097168 | tf_op jit(solution)/shard_map/all_gather | solution.py:45
  681.4 60.2 %all-reduce.25.cloned.1.call-done = f32[256,128]{0,1:T(8,128)} async-done(((f32[256,128]{0,1:T(8,128)}), f32[256,128]{0,1:T(8,128)}) %all-reduce.25.cloned.1.call-update) | async-done | bytes 131088 | tf_op jit(solution)/shard_map/psum | solution.py:42
  744.4 46.2 %all-gather.25.cloned.1.call-done = bf16[4096,256]{0,1:T(8,128)(2,1)} async-done(((bf16[256,256]{0,1:T(8,128)(2,1)}), bf16[4096,256]{0,1:T(8,128)(2,1)}) %all-gather.25.cloned.1.call-update) | async-done | bytes 2097168 | tf_op jit(solution)/shard_map/all_gather | solution.py:45
  792.6 60.1 %all-reduce.27.cloned.1.call-done = f32[256,128]{0,1:T(8,128)} async-done(((f32[256,128]{0,1:T(8,128)}), f32[256,128]{0,1:T(8,128)}) %all-reduce.27.cloned.1.call-update) | async-done | bytes 131088 | tf_op jit(solution)/shard_map/psum | solution.py:42
  854.7 46.6 %all-gather.27.cloned.1.call-done = bf16[4096,256]{0,1:T(8,128)(2,1)} async-done(((bf16[256,256]{0,1:T(8,128)(2,1)}), bf16[4096,256]{0,1:T(8,128)(2,1)}) %all-gather.27.cloned.1.call-update) | async-done | bytes 2097168 | tf_op jit(solution)/shard_map/all_gather | solution.py:45
  906.3 59.3 %all-reduce.29.cloned.1.call-done = f32[256,128]{0,1:T(8,128)} async-done(((f32[256,128]{0,1:T(8,128)}), f32[256,128]{0,1:T(8,128)}) %all-reduce.29.cloned.1.call-update) | async-done | bytes 131088 | tf_op jit(solution)/shard_map/psum | solution.py:42
  968.1 46.2 %all-gather.29.cloned.1.call-done = bf16[4096,256]{0,1:T(8,128)(2,1)} async-done(((bf16[256,256]{0,1:T(8,128)(2,1)}), bf16[4096,256]{0,1:T(8,128)(2,1)}) %all-gather.29.cloned.1.call-update) | async-done | bytes 2097168 | tf_op jit(solution)/shard_map/all_gather | solution.py:45
  1016.3 60.2 %all-reduce.31.cloned.1.call-done = f32[256,128]{0,1:T(8,128)} async-done(((f32[256,128]{0,1:T(8,128)}), f32[256,128]{0,1:T(8,128)}) %all-reduce.31.cloned.1.call-update) | async-done | bytes 131088 | tf_op jit(solution)/shard_map/psum | solution.py:42
  1079.2 46.2 %all-gather.31.cloned.1.call-done = bf16[4096,256]{0,1:T(8,128)(2,1)} async-done(((bf16[256,256]{0,1:T(8,128)(2,1)}), bf16[4096,256]{0,1:T(8,128)(2,1)}) %all-gather.31.cloned.1.call-update) | async-done | bytes 2097168 | tf_op jit(solution)/shard_map/all_gather | solution.py:45
  1127.3 60.2 %all-reduce.33.cloned.1.call-done = f32[256,128]{0,1:T(8,128)} async-done(((f32[256,128]{0,1:T(8,128)}), f32[256,128]{0,1:T(8,128)}) %all-reduce.33.cloned.1.call-update) | async-done | bytes 131088 | tf_op jit(solution)/shard_map/psum | solution.py:42
  1190.4 46.2 %all-gather.33.cloned.1.call-done = bf16[4096,256]{0,1:T(8,128)(2,1)} async-done(((bf16[256,256]{0,1:T(8,128)(2,1)}), bf16[4096,256]{0,1:T(8,128)(2,1)}) %all-gather.33.cloned.1.call-update) | async-done | bytes 2097168 | tf_op jit(solution)/shard_map/all_gather | solution.py:45
  1238.6 60.2 %all-reduce.35.cloned.1.call-done = f32[256,128]{0,1:T(8,128)} async-done(((f32[256,128]{0,1:T(8,128)}), f32[256,128]{0,1:T(8,128)}) %all-reduce.35.cloned.1.call-update) | async-done | bytes 131088 | tf_op jit(solution)/shard_map/psum | solution.py:42
  1313.2 34.3 %all-gather.35.cloned.1.call-done = bf16[4096,256]{0,1:T(8,128)(2,1)} async-done(((bf16[256,256]{0,1:T(8,128)(2,1)}), bf16[4096,256]{0,1:T(8,128)(2,1)}) %all-gather.35.cloned.1.call-update) | async-done | bytes 2097168 | tf_op jit(solution)/shard_map/all_gather | solution.py:45
  (164 shorter events, 115.4 us)
Async XLA Ops:
  10.8 111.4 %all-gather.13.cloned.1.call-start = ((), (), s32[]{:S(2)}) async-start(), calls=%async_computation.2 | async-start | bytes 2228224 | tf_op jit(solution)/shard_map/all_gather | solution.py:45
  75.9 108.5 %all-reduce.15.cloned.1.call-start = ((), (), s32[]{:S(2)}) async-start(), calls=%async_computation.3 | async-start | bytes 262144 | tf_op jit(solution)/shard_map/psum | solution.py:42
  124.1 109.1 %all-gather.15.cloned.1.call-start = ((), (), s32[]{:S(2)}) async-start(), calls=%async_computation.4 | async-start | bytes 2228224 | tf_op jit(solution)/shard_map/all_gather | solution.py:45
  187.0 108.3 %all-reduce.17.cloned.1.call-start = ((), (), s32[]{:S(2)}) async-start(), calls=%async_computation.5 | async-start | bytes 262144 | tf_op jit(solution)/shard_map/psum | solution.py:42
  235.2 109.1 %all-gather.17.cloned.1.call-start = ((), (), s32[]{:S(2)}) async-start(), calls=%async_computation.6 | async-start | bytes 2228224 | tf_op jit(solution)/shard_map/all_gather | solution.py:45
  298.1 108.4 %all-reduce.19.cloned.1.call-start = ((), (), s32[]{:S(2)}) async-start(), calls=%async_computation.7 | async-start | bytes 262144 | tf_op jit(solution)/shard_map/psum | solution.py:42
  346.2 109.1 %all-gather.19.cloned.1.call-start = ((), (), s32[]{:S(2)}) async-start(), calls=%async_computation.8 | async-start | bytes 2228224 | tf_op jit(solution)/shard_map/all_gather | solution.py:45
  408.2 111.3 %all-reduce.21.cloned.1.call-start = ((), (), s32[]{:S(2)}) async-start(), calls=%async_computation.9 | async-start | bytes 262144 | tf_op jit(solution)/shard_map/psum | solution.py:42
  460.1 108.2 %all-gather.21.cloned.1.call-start = ((), (), s32[]{:S(2)}) async-start(), calls=%async_computation.10 | async-start | bytes 2228224 | tf_op jit(solution)/shard_map/all_gather | solution.py:45
  522.1 108.5 %all-reduce.23.cloned.1.call-start = ((), (), s32[]{:S(2)}) async-start(), calls=%async_computation.11 | async-start | bytes 262144 | tf_op jit(solution)/shard_map/psum | solution.py:42
  570.3 109.1 %all-gather.23.cloned.1.call-start = ((), (), s32[]{:S(2)}) async-start(), calls=%async_computation.12 | async-start | bytes 2228224 | tf_op jit(solution)/shard_map/all_gather | solution.py:45
  633.1 108.4 %all-reduce.25.cloned.1.call-start = ((), (), s32[]{:S(2)}) async-start(), calls=%async_computation.13 | async-start | bytes 262144 | tf_op jit(solution)/shard_map/psum | solution.py:42
  681.3 109.3 %all-gather.25.cloned.1.call-start = ((), (), s32[]{:S(2)}) async-start(), calls=%async_computation.14 | async-start | bytes 2228224 | tf_op jit(solution)/shard_map/all_gather | solution.py:45
  744.3 108.3 %all-reduce.27.cloned.1.call-start = ((), (), s32[]{:S(2)}) async-start(), calls=%async_computation.15 | async-start | bytes 262144 | tf_op jit(solution)/shard_map/psum | solution.py:42
  792.5 108.8 %all-gather.27.cloned.1.call-start = ((), (), s32[]{:S(2)}) async-start(), calls=%async_computation.16 | async-start | bytes 2228224 | tf_op jit(solution)/shard_map/all_gather | solution.py:45
  854.4 111.2 %all-reduce.29.cloned.1.call-start = ((), (), s32[]{:S(2)}) async-start(), calls=%async_computation.17 | async-start | bytes 262144 | tf_op jit(solution)/shard_map/psum | solution.py:42
  906.1 108.2 %all-gather.29.cloned.1.call-start = ((), (), s32[]{:S(2)}) async-start(), calls=%async_computation.18 | async-start | bytes 2228224 | tf_op jit(solution)/shard_map/all_gather | solution.py:45
  968.1 108.4 %all-reduce.31.cloned.1.call-start = ((), (), s32[]{:S(2)}) async-start(), calls=%async_computation.19 | async-start | bytes 262144 | tf_op jit(solution)/shard_map/psum | solution.py:42
  1016.2 109.1 %all-gather.31.cloned.1.call-start = ((), (), s32[]{:S(2)}) async-start(), calls=%async_computation.20 | async-start | bytes 2228224 | tf_op jit(solution)/shard_map/all_gather | solution.py:45
  1079.1 108.5 %all-reduce.33.cloned.1.call-start = ((), (), s32[]{:S(2)}) async-start(), calls=%async_computation.21 | async-start | bytes 262144 | tf_op jit(solution)/shard_map/psum | solution.py:42
  1127.3 109.3 %all-gather.33.cloned.1.call-start = ((), (), s32[]{:S(2)}) async-start(), calls=%async_computation.22 | async-start | bytes 2228224 | tf_op jit(solution)/shard_map/all_gather | solution.py:45
  1190.3 108.5 %all-reduce.35.cloned.1.call-start = ((), (), s32[]{:S(2)}) async-start(), calls=%async_computation.23 | async-start | bytes 262144 | tf_op jit(solution)/shard_map/psum | solution.py:42
  1238.5 109.0 %all-gather.35.cloned.1.call-start = ((), (), s32[]{:S(2)}) async-start(), calls=%async_computation.24 | async-start | bytes 2228224 | tf_op jit(solution)/shard_map/all_gather | solution.py:45
  1300.5 87.6 %reduce-scatter.2.cloned.1.call-start = ((), (), s32[]{:S(2)}) async-start(), calls=%async_computation.25 | async-start | bytes 1769472 | tf_op jit(solution)/shard_map/reduce_scatter | solution.py:100
  (14 other events, 1878.5 us)
Sparse Core Ops, SparseCore 0:
  11.0 62.3 all-reduce.12
  76.1 46.0 all-gather.12
  125.1 59.2 all-reduce.14
  187.1 46.0 all-gather.14
  236.0 59.2 all-reduce.16
  298.2 46.0 all-gather.16
  347.2 59.2 all-reduce.18
  409.2 46.0 all-gather.18
  460.2 59.2 all-reduce.20
  522.2 46.0 all-gather.20
  571.2 59.2 all-reduce.22
  633.3 46.0 all-gather.22
  682.3 59.2 all-reduce.24
  744.4 46.0 all-gather.24
  793.3 59.2 all-reduce.26
  855.2 46.0 all-gather.26
  906.2 59.2 all-reduce.28
  968.2 46.0 all-gather.28
  1017.2 59.2 all-reduce.30
  1079.2 46.0 all-gather.30
  1128.3 59.2 all-reduce.32
  1190.4 46.0 all-gather.32
  1239.5 59.2 all-reduce.34
  1301.3 46.0 all-gather.34
  (1 shorter events, 32.2 us)
where the time goes:
time: 1400 us
  waiting for transfers between devices  1300 us (93%)
  other arithmetic  37.5 us (3%)
  matrix products  28.1 us (2%)
  local copies, waits for them, and re-layouts  17.3 us (1%)
  between operations  14.6 us (1%)
    psum x12, waiting for transfers between devices, reduce_rows(): return lax.psum(partial_value, 'col')  723 us
    all_gather x12, waiting for transfers between devices, spread_rows(): return lax.all_gather(values, 'row', axis=0, tiled=True)  544 us
    reduce_scatter x1, waiting for transfers between devices, body(): lax.psum_scatter(fold_pair(jnp.dot(z_flat, picked, preferred_element_type...  31.1 us
  transfers between devices with their start and end apart: 25, of which 25 were waited for; matrix products, arithmetic and copies ran while one was open for 1% of the time, Pallas kernels for 0%

commit v1 on v0

--- a/solution.py
+++ b/solution.py
@@ -39,7 +39,7 @@
     local_start = row_idx * row_block
 
     def reduce_rows(partial_value):
-        return lax.psum(partial_value, "col")
+        return jnp.sum(lax.all_gather(partial_value, "col"), axis=0)
 
     def spread_rows(values):
         return lax.all_gather(values, "row", axis=0, tiled=True)

time: 1400 us -> 964 us (0.69)
  waiting for transfers between devices: 1300 us -> 861 us
  local copies, waits for them, and re-layouts: 17.3 us -> 36.2 us
  other arithmetic: 37.5 us -> 21.3 us
    psum x12 -> x0, waiting for transfers between devices: 723 us -> none  [reduce_rows(): return lax.psum(partial_value, 'col')]
    all_gather x0 -> x12, waiting for transfers between devices: none -> 276 us  [reduce_rows(): return jnp.sum(lax.all_gather(partial_value, 'col'), axis=0)]
    unnamed x32, local copies, waits for them, and re-layouts: 13.9 us -> 32.8 us
  transfers between devices with their start and end apart: 25 -> 25, of which waited for: 25 -> 25; matrix products, arithmetic and copies ran while one was open for 1% -> 2% of each run, Pallas kernels for 0% -> 0%
where the time goes in v1:
time: 964 us; the launch traced here: 962 us
  waiting for transfers between devices  861 us (89%)
  local copies, waits for them, and re-layouts  36.2 us (4%)
  matrix products  28.1 us (3%)
  other arithmetic  21.3 us (2%)
  between operations  14.7 us (2%)
    all_gather x12, waiting for transfers between devices, spread_rows(): return lax.all_gather(values, 'row', axis=0, tiled=True)  553 us
    all_gather x12, waiting for transfers between devices, reduce_rows(): return jnp.sum(lax.all_gather(partial_value, 'col'), axis=0)  276 us
    unnamed x32, local copies, waits for them, and re-layouts  32.8 us
    reduce_scatter x1, waiting for transfers between devices, body(): lax.psum_scatter(fold_pair(jnp.dot(z_flat, picked, preferred_element_type...  31.1 us
  transfers between devices with their start and end apart: 25, of which 25 were waited for; matrix products, arithmetic and copies ran while one was open for 2% of the time, Pallas kernels for 0%

profile of v1, /device:TPU:0, one launch (start us, length us, event | category | flops | bytes accessed | tf_op | source)
XLA Modules:
  0.0 962.5 jit_solution(871236657500039584)
XLA Ops:
  11.0 25.7 %all-gather.61.cloned.1.call-done = f32[2048,128]{0,1:T(8,128)} async-done(((f32[256,128]{0,1:T(8,128)}), f32[2048,128]{0,1:T(8,128)}) %all-gather.61.cloned.1.call-update) | async-done | bytes 1048592 | tf_op jit(solution)/shard_map/all_gather | solution.py:42
  39.4 47.2 %all-gather.37.cloned.1.call-done = bf16[4096,256]{0,1:T(8,128)(2,1)} async-done(((bf16[256,256]{0,1:T(8,128)(2,1)}), bf16[4096,256]{0,1:T(8,128)(2,1)}) %all-gather.37.cloned.1.call-update) | async-done | bytes 2097168 | tf_op jit(solution)/shard_map/all_gather | solution.py:45
  88.6 22.9 %all-gather.63.cloned.1.call-done = f32[2048,128]{0,1:T(8,128)} async-done(((f32[256,128]{0,1:T(8,128)}), f32[2048,128]{0,1:T(8,128)}) %all-gather.63.cloned.1.call-update) | async-done | bytes 1048592 | tf_op jit(solution)/shard_map/all_gather | solution.py:42
  114.1 47.2 %all-gather.39.cloned.1.call-done = bf16[4096,256]{0,1:T(8,128)(2,1)} async-done(((bf16[256,256]{0,1:T(8,128)(2,1)}), bf16[4096,256]{0,1:T(8,128)(2,1)}) %all-gather.39.cloned.1.call-update) | async-done | bytes 2097168 | tf_op jit(solution)/shard_map/all_gather | solution.py:45
  163.3 22.7 %all-gather.65.cloned.1.call-done = f32[2048,128]{0,1:T(8,128)} async-done(((f32[256,128]{0,1:T(8,128)}), f32[2048,128]{0,1:T(8,128)}) %all-gather.65.cloned.1.call-update) | async-done | bytes 1048592 | tf_op jit(solution)/shard_map/all_gather | solution.py:42
  188.7 47.2 %all-gather.41.cloned.1.call-done = bf16[4096,256]{0,1:T(8,128)(2,1)} async-done(((bf16[256,256]{0,1:T(8,128)(2,1)}), bf16[4096,256]{0,1:T(8,128)(2,1)}) %all-gather.41.cloned.1.call-update) | async-done | bytes 2097168 | tf_op jit(solution)/shard_map/all_gather | solution.py:45
  237.9 22.8 %all-gather.67.cloned.1.call-done = f32[2048,128]{0,1:T(8,128)} async-done(((f32[256,128]{0,1:T(8,128)}), f32[2048,128]{0,1:T(8,128)}) %all-gather.67.cloned.1.call-update) | async-done | bytes 1048592 | tf_op jit(solution)/shard_map/all_gather | solution.py:42
  263.5 47.2 %all-gather.43.cloned.1.call-done = bf16[4096,256]{0,1:T(8,128)(2,1)} async-done(((bf16[256,256]{0,1:T(8,128)(2,1)}), bf16[4096,256]{0,1:T(8,128)(2,1)}) %all-gather.43.cloned.1.call-update) | async-done | bytes 2097168 | tf_op jit(solution)/shard_map/all_gather | solution.py:45
  315.7 22.5 %all-gather.69.cloned.1.call-done = f32[2048,128]{0,1:T(8,128)} async-done(((f32[256,128]{0,1:T(8,128)}), f32[2048,128]{0,1:T(8,128)}) %all-gather.69.cloned.1.call-update) | async-done | bytes 1048592 | tf_op jit(solution)/shard_map/all_gather | solution.py:42
  340.8 47.2 %all-gather.45.cloned.1.call-done = bf16[4096,256]{0,1:T(8,128)(2,1)} async-done(((bf16[256,256]{0,1:T(8,128)(2,1)}), bf16[4096,256]{0,1:T(8,128)(2,1)}) %all-gather.45.cloned.1.call-update) | async-done | bytes 2097168 | tf_op jit(solution)/shard_map/all_gather | solution.py:45
  390.0 22.9 %all-gather.71.cloned.1.call-done = f32[2048,128]{0,1:T(8,128)} async-done(((f32[256,128]{0,1:T(8,128)}), f32[2048,128]{0,1:T(8,128)}) %all-gather.71.cloned.1.call-update) | async-done | bytes 1048592 | tf_op jit(solution)/shard_map/all_gather | solution.py:42
  415.5 47.2 %all-gather.47.cloned.1.call-done = bf16[4096,256]{0,1:T(8,128)(2,1)} async-done(((bf16[256,256]{0,1:T(8,128)(2,1)}), bf16[4096,256]{0,1:T(8,128)(2,1)}) %all-gather.47.cloned.1.call-update) | async-done | bytes 2097168 | tf_op jit(solution)/shard_map/all_gather | solution.py:45
  464.6 22.9 %all-gather.73.cloned.1.call-done = f32[2048,128]{0,1:T(8,128)} async-done(((f32[256,128]{0,1:T(8,128)}), f32[2048,128]{0,1:T(8,128)}) %all-gather.73.cloned.1.call-update) | async-done | bytes 1048592 | tf_op jit(solution)/shard_map/all_gather | solution.py:42
  490.3 47.2 %all-gather.49.cloned.1.call-done = bf16[4096,256]{0,1:T(8,128)(2,1)} async-done(((bf16[256,256]{0,1:T(8,128)(2,1)}), bf16[4096,256]{0,1:T(8,128)(2,1)}) %all-gather.49.cloned.1.call-update) | async-done | bytes 2097168 | tf_op jit(solution)/shard_map/all_gather | solution.py:45
  539.4 22.7 %all-gather.75.cloned.1.call-done = f32[2048,128]{0,1:T(8,128)} async-done(((f32[256,128]{0,1:T(8,128)}), f32[2048,128]{0,1:T(8,128)}) %all-gather.75.cloned.1.call-update) | async-done | bytes 1048592 | tf_op jit(solution)/shard_map/all_gather | solution.py:42
  565.1 46.9 %all-gather.51.cloned.1.call-done = bf16[4096,256]{0,1:T(8,128)(2,1)} async-done(((bf16[256,256]{0,1:T(8,128)(2,1)}), bf16[4096,256]{0,1:T(8,128)(2,1)}) %all-gather.51.cloned.1.call-update) | async-done | bytes 2097168 | tf_op jit(solution)/shard_map/all_gather | solution.py:45
  642.1 47.2 %all-gather.53.cloned.1.call-done = bf16[4096,256]{0,1:T(8,128)(2,1)} async-done(((bf16[256,256]{0,1:T(8,128)(2,1)}), bf16[4096,256]{0,1:T(8,128)(2,1)}) %all-gather.53.cloned.1.call-update) | async-done | bytes 2097168 | tf_op jit(solution)/shard_map/all_gather | solution.py:45
  691.3 22.9 %all-gather.79.cloned.1.call-done = f32[2048,128]{0,1:T(8,128)} async-done(((f32[256,128]{0,1:T(8,128)}), f32[2048,128]{0,1:T(8,128)}) %all-gather.79.cloned.1.call-update) | async-done | bytes 1048592 | tf_op jit(solution)/shard_map/all_gather | solution.py:42
  716.8 47.2 %all-gather.55.cloned.1.call-done = bf16[4096,256]{0,1:T(8,128)(2,1)} async-done(((bf16[256,256]{0,1:T(8,128)(2,1)}), bf16[4096,256]{0,1:T(8,128)(2,1)}) %all-gather.55.cloned.1.call-update) | async-done | bytes 2097168 | tf_op jit(solution)/shard_map/all_gather | solution.py:45
  765.9 22.9 %all-gather.81.cloned.1.call-done = f32[2048,128]{0,1:T(8,128)} async-done(((f32[256,128]{0,1:T(8,128)}), f32[2048,128]{0,1:T(8,128)}) %all-gather.81.cloned.1.call-update) | async-done | bytes 1048592 | tf_op jit(solution)/shard_map/all_gather | solution.py:42
  791.5 47.2 %all-gather.57.cloned.1.call-done = bf16[4096,256]{0,1:T(8,128)(2,1)} async-done(((bf16[256,256]{0,1:T(8,128)(2,1)}), bf16[4096,256]{0,1:T(8,128)(2,1)}) %all-gather.57.cloned.1.call-update) | async-done | bytes 2097168 | tf_op jit(solution)/shard_map/all_gather | solution.py:45
  840.7 22.9 %all-gather.83.cloned.1.call-done = f32[2048,128]{0,1:T(8,128)} async-done(((f32[256,128]{0,1:T(8,128)}), f32[2048,128]{0,1:T(8,128)}) %all-gather.83.cloned.1.call-update) | async-done | bytes 1048592 | tf_op jit(solution)/shard_map/all_gather | solution.py:42
  878.9 34.6 %all-gather.59.cloned.1.call-done = bf16[4096,256]{0,1:T(8,128)(2,1)} async-done(((bf16[256,256]{0,1:T(8,128)(2,1)}), bf16[4096,256]{0,1:T(8,128)(2,1)}) %all-gather.59.cloned.1.call-update) | async-done | bytes 2097168 | tf_op jit(solution)/shard_map/all_gather | solution.py:45
  923.0 31.1 %reduce-scatter.2.cloned.1.call-done = f32[384,128]{0,1:T(8,128)} async-done(((f32[3072,128]{0,1:T(8,128)}), f32[384,128]{0,1:T(8,128)}) %reduce-scatter.2.cloned.1.call-update) | async-done | bytes 196624 | tf_op jit(solution)/shard_map/reduce_scatter | solution.py:100
  (176 shorter events, 109.5 us)
Async XLA Ops:
  10.8 75.8 %all-gather.37.cloned.1.call-start = ((), (), s32[]{:S(2)}) async-start(), calls=%async_computation.1 | async-start | bytes 2228224 | tf_op jit(solution)/shard_map/all_gather | solution.py:45
  39.4 72.1 %all-gather.63.cloned.1.call-start = ((), (), s32[]{:S(2)}) async-start(), calls=%async_computation.15 | async-start | bytes 1179648 | tf_op jit(solution)/shard_map/all_gather | solution.py:42
  88.6 72.7 %all-gather.39.cloned.1.call-start = ((), (), s32[]{:S(2)}) async-start(), calls=%async_computation.2 | async-start | bytes 2228224 | tf_op jit(solution)/shard_map/all_gather | solution.py:45
  114.0 71.9 %all-gather.65.cloned.1.call-start = ((), (), s32[]{:S(2)}) async-start(), calls=%async_computation.16 | async-start | bytes 1179648 | tf_op jit(solution)/shard_map/all_gather | solution.py:42
  163.2 72.7 %all-gather.41.cloned.1.call-start = ((), (), s32[]{:S(2)}) async-start(), calls=%async_computation.3 | async-start | bytes 2228224 | tf_op jit(solution)/shard_map/all_gather | solution.py:45
  188.7 72.1 %all-gather.67.cloned.1.call-start = ((), (), s32[]{:S(2)}) async-start(), calls=%async_computation.17 | async-start | bytes 1179648 | tf_op jit(solution)/shard_map/all_gather | solution.py:42
  237.8 72.9 %all-gather.43.cloned.1.call-start = ((), (), s32[]{:S(2)}) async-start(), calls=%async_computation.4 | async-start | bytes 2228224 | tf_op jit(solution)/shard_map/all_gather | solution.py:45
  263.5 74.7 %all-gather.69.cloned.1.call-start = ((), (), s32[]{:S(2)}) async-start(), calls=%async_computation.18 | async-start | bytes 1179648 | tf_op jit(solution)/shard_map/all_gather | solution.py:42
  315.5 72.5 %all-gather.45.cloned.1.call-start = ((), (), s32[]{:S(2)}) async-start(), calls=%async_computation.5 | async-start | bytes 2228224 | tf_op jit(solution)/shard_map/all_gather | solution.py:45
  340.8 72.1 %all-gather.71.cloned.1.call-start = ((), (), s32[]{:S(2)}) async-start(), calls=%async_computation.19 | async-start | bytes 1179648 | tf_op jit(solution)/shard_map/all_gather | solution.py:42
  389.9 72.7 %all-gather.47.cloned.1.call-start = ((), (), s32[]{:S(2)}) async-start(), calls=%async_computation.6 | async-start | bytes 2228224 | tf_op jit(solution)/shard_map/all_gather | solution.py:45
  415.4 72.1 %all-gather.73.cloned.1.call-start = ((), (), s32[]{:S(2)}) async-start(), calls=%async_computation.20 | async-start | bytes 1179648 | tf_op jit(solution)/shard_map/all_gather | solution.py:42
  464.6 72.9 %all-gather.49.cloned.1.call-start = ((), (), s32[]{:S(2)}) async-start(), calls=%async_computation.7 | async-start | bytes 2228224 | tf_op jit(solution)/shard_map/all_gather | solution.py:45
  490.2 71.9 %all-gather.75.cloned.1.call-start = ((), (), s32[]{:S(2)}) async-start(), calls=%async_computation.21 | async-start | bytes 1179648 | tf_op jit(solution)/shard_map/all_gather | solution.py:42
  539.4 72.7 %all-gather.51.cloned.1.call-start = ((), (), s32[]{:S(2)}) async-start(), calls=%async_computation.8 | async-start | bytes 2228224 | tf_op jit(solution)/shard_map/all_gather | solution.py:45
  564.8 74.7 %all-gather.77.cloned.1.call-start = ((), (), s32[]{:S(2)}) async-start(), calls=%async_computation.22 | async-start | bytes 1179648 | tf_op jit(solution)/shard_map/all_gather | solution.py:42
  616.8 72.5 %all-gather.53.cloned.1.call-start = ((), (), s32[]{:S(2)}) async-start(), calls=%async_computation.9 | async-start | bytes 2228224 | tf_op jit(solution)/shard_map/all_gather | solution.py:45
  642.1 72.1 %all-gather.79.cloned.1.call-start = ((), (), s32[]{:S(2)}) async-start(), calls=%async_computation.23 | async-start | bytes 1179648 | tf_op jit(solution)/shard_map/all_gather | solution.py:42
  691.2 72.7 %all-gather.55.cloned.1.call-start = ((), (), s32[]{:S(2)}) async-start(), calls=%async_computation.10 | async-start | bytes 2228224 | tf_op jit(solution)/shard_map/all_gather | solution.py:45
  716.7 72.1 %all-gather.81.cloned.1.call-start = ((), (), s32[]{:S(2)}) async-start(), calls=%async_computation.24 | async-start | bytes 1179648 | tf_op jit(solution)/shard_map/all_gather | solution.py:42
  765.9 72.9 %all-gather.57.cloned.1.call-start = ((), (), s32[]{:S(2)}) async-start(), calls=%async_computation.11 | async-start | bytes 2228224 | tf_op jit(solution)/shard_map/all_gather | solution.py:45
  791.5 72.1 %all-gather.83.cloned.1.call-start = ((), (), s32[]{:S(2)}) async-start(), calls=%async_computation.25 | async-start | bytes 1179648 | tf_op jit(solution)/shard_map/all_gather | solution.py:42
  840.7 72.8 %all-gather.59.cloned.1.call-start = ((), (), s32[]{:S(2)}) async-start(), calls=%async_computation.12 | async-start | bytes 2228224 | tf_op jit(solution)/shard_map/all_gather | solution.py:45
  866.2 87.9 %reduce-scatter.2.cloned.1.call-start = ((), (), s32[]{:S(2)}) async-start(), calls=%async_computation.13 | async-start | bytes 1769472 | tf_op jit(solution)/shard_map/reduce_scatter | solution.py:100
  (8 other events, 221.9 us)
Sparse Core Ops, SparseCore 0:
  10.9 25.7 all-gather.60
  39.5 47.0 all-gather.36
  88.9 22.5 all-gather.62
  114.2 47.0 all-gather.38
  163.4 22.5 all-gather.64
  188.8 47.0 all-gather.40
  238.2 22.5 all-gather.66
  263.6 47.0 all-gather.42
  315.6 22.5 all-gather.68
  340.9 47.0 all-gather.44
  390.3 22.5 all-gather.70
  415.5 47.0 all-gather.46
  464.9 22.5 all-gather.72
  490.3 47.0 all-gather.48
  539.6 22.5 all-gather.74
  564.9 47.0 all-gather.50
  642.2 47.0 all-gather.52
  691.6 22.5 all-gather.78
  716.8 47.0 all-gather.54
  766.2 22.5 all-gather.80
  791.6 47.0 all-gather.56
  841.0 22.5 all-gather.82
  866.4 47.0 all-gather.58
  921.9 32.2 reduce-scatter.1
  (1 shorter events, 22.5 us)
